TPU v7x, 32 devices: a whole 2x2x4 slice. The times are simulated.
32 devices in a mesh: gen: 4 (over x, core), join: 8 (over z, y).
Axes of the slice: x: 2, y: 2, z: 4, core: 2. Of those that a mesh axis runs over, the one named last changes fastest.
Arguments:
- src_emb: bfloat16 [65536, 512], P(('gen', 'join')), may hold values from -64 to 64
- counts: int32 [32, 32], P(('gen', 'join')), may hold values from 0 to 64, as said below
Outputs:
- dup_weight: float32 [65536], P(('gen', 'join'))
Inputs may be any that keep to these rules, and one draw needn't show every extreme that they name: Slot c of source s for owner o is live when c < counts[s, o]; in every draw some owner receives 64 live slots from every source.
All inputs are finite; a program needn't handle non-finite values.
Results may differ from a plain program's by a relative error of at most 0.0016.
Values may be sent and summed in bfloat16 or wider, within the bound.
A program may use at most 64 MiB of HBM per device.

v0:
```python
import math

import jax
import jax.numpy as jnp
from jax import lax
from jax.sharding import PartitionSpec as P

ROUNDS = 3


def shifted(block, axis, distance):
    devices = range(lax.axis_size(axis))
    route = [((i - distance) % len(devices), i) for i in devices]
    return lax.ppermute(block, axis, route)


def tile_sums(left_rows, left_live, right_rows, right_live):
    row_count = left_rows.shape[0]
    piece_rows = min(512, row_count)
    pieces = row_count // piece_rows

    def one_piece(col_total, operands):
        piece_block, piece_live = operands
        scores = lax.dot_general(
            piece_block, right_rows, (((1,), (1,)), ((), ())), preferred_element_type=jnp.float32
        )
        kernel = jnp.exp(8.0 * (scores - 1.0))
        return (
            col_total + jnp.sum(kernel * piece_live[:, None], axis=0),
            jnp.sum(kernel * right_live[None, :], axis=1),
        )

    start_total = jnp.zeros((right_rows.shape[0],), jnp.float32)
    col_sums, row_sums = lax.scan(
        one_piece,
        start_total,
        (
            left_rows.reshape(pieces, piece_rows, left_rows.shape[1]),
            left_live.reshape(pieces, piece_rows),
        ),
    )
    return (row_sums.reshape(row_count), col_sums)


def body(src_emb, counts):
    values = src_emb.astype(jnp.float32)
    width = values.shape[1]
    unit = (
        values
        * lax.rsqrt(jnp.mean(values * values, axis=1, keepdims=True) + 1e-06)
        / math.sqrt(width)
    ).astype(jnp.bfloat16)
    nodes = lax.axis_size(("gen", "join"))
    block_rows = unit.shape[0]
    slots = block_rows // nodes
    received, got_counts = (
        lax.all_to_all(
            unit.reshape(nodes, slots, width),
            ("gen", "join"),
            split_axis=0,
            concat_axis=0,
            tiled=True,
        ),
        lax.all_to_all(
            counts.reshape(nodes), ("gen", "join"), split_axis=0, concat_axis=0, tiled=True
        ),
    )
    owned = received.reshape(block_rows, width)
    slot_index = lax.broadcasted_iota(jnp.int32, (nodes, slots), 1)
    live = (slot_index < got_counts.reshape(nodes, 1)).astype(jnp.float32).reshape(block_rows)
    live_wire = live.astype(jnp.bfloat16)
    density = tile_sums(owned, live, owned, live)[0]
    for shift_by in range(1, ROUNDS + 1):
        other_rows, other_flags = shifted((owned, live_wire), "join", shift_by)
        row_sums, col_sums = tile_sums(owned, live, other_rows, other_flags.astype(jnp.float32))
        density = density + row_sums + shifted(col_sums, "join", -shift_by)
    return live / (density + 1.0 - live)


def solution(mesh):
    in_specs = (P(("gen", "join"), None), P(("gen", "join"), None))
    out_specs = P(("gen", "join"))
    return jax.shard_map(body, mesh=mesh, in_specs=in_specs, out_specs=out_specs, check_vma=False)
```

profile of v0, /device:TPU:1, one launch (start us, length us, event | category | flops | bytes accessed | tf_op | source)
XLA Modules:
  0.0 270.1 jit_solution(8621658523053602905)
XLA Ops:
  1.5 7.1 %all-to-all-start = ((s32[32,1,1]{2,1,0:T(1,128)}), s32[32,1,1]{2,1,0:T(1,128)S(1)}, u32[]{:S(2)}, u32[]{:S(2)}) async-start(s32[32,1,1]{2,1,0:T(1,128)} %copy.4), calls=%async_computation | async-start | bytes 32768 | tf_op jit(solution)/shard_map/all_to_all | solution.py:64
  8.6 2.1 fusion.18
  10.7 1.8 fusion.20
  12.5 2.8 %all-to-all-done = s32[32,1,1]{2,1,0:T(1,128)S(1)} async-done(((s32[32,1,1]{2,1,0:T(1,128)}), s32[32,1,1]{2,1,0:T(1,128)S(1)}, u32[]{:S(2)}, u32[]{:S(2)}) %all-to-all-start) | async-done | bytes 160 | tf_op jit(solution)/shard_map/all_to_all | solution.py:64
  15.3 3.7 %all-to-all-start.1 = ((bf16[32,64,512]{2,1,0:T(8,128)(2,1)}), bf16[32,64,512]{2,1,0:T(8,128)(2,1)}, u32[]{:S(2)}, u32[]{:S(2)}) async-start(bf16[32,64,512]{2,1,0:T(8,128)(2,1)} %bitcast.70), calls=%async_computation.1 | async-start | bytes 4194304 | tf_op jit(solution)/shard_map/all_to_all | solution.py:57
  22.7 2.2 collective-permute-start.7
  25.0 32.9 %collective-permute-done.1 = bf16[2048]{0:T(1024)(128)(2,1)S(1)} collective-permute-done((bf16[2048]{0:T(1024)(128)(2,1)S(1)}, bf16[2048]{0:T(1024)(128)(2,1)S(1)}, u32[]{:S(2)}, u32[]{:S(2)}) %collective-permute-start.1) | collective-permute-done | bytes 4128 | tf_op jit(solution)/shard_map/ppermute | solution.py:14
  57.9 10.6 %collective-permute-done.7 = bf16[2048]{0:T(1024)(128)(2,1)S(1)} collective-permute-done((bf16[2048]{0:T(1024)(128)(2,1)S(1)}, bf16[2048]{0:T(1024)(128)(2,1)S(1)}, u32[]{:S(2)}, u32[]{:S(2)}) %collective-permute-start.7) | collective-permute-done | bytes 4128 | tf_op jit(solution)/shard_map/ppermute | solution.py:14
  69.7 1.7 collective-permute-start.6
  71.4 13.8 %while.58 = (s32[]{:T(128)}, f32[4,512]{1,0:T(4,128)S(1)}, bf16[4,512,512]{2,1,0:T(8,128)(2,1)}, bf16[2048,512]{1,0:T(8,128)(2,1)}, s32[32]{0:T(128)S(1)}, /*index=5*/s32[]{:T(128)}, s32[]{:T(128)}) while((s32[]{:T(128)}, f32[4,512]{1,0:T(4,128)S(1)}, bf16[4,512,512]{2,1,0:T(8,128)(2,1)}, bf16[2048,512]{1,0:T(8,128)(2,1)}, ...), condition=%wide.region_3.4_spmd.clone, body=%wide.region_1.3_spmd.clone.sunk | while | flops 1077939712 | bytes 2661073 | solution.py:34
  71.6 3.2 %multiply_reduce_fusion.11 = f32[512]{0:T(512)S(1)} fusion(bf16[2048,512]{1,0:T(8,128)(2,1)} %get-tuple-element.733, f32[2048]{0:T(1024)S(1)} %mul.233, bf16[4,512,512]{2,1,0:T(8,128)(2,1)} %get-tuple-element.732, s32[]{:T(128)} %get-tuple-element.723), kind=kOutput, calls=%fused_computation.1.clone.1 | convolution fusion | flops 1077935616 | bytes 2632192 | tf_op jit(solution)/shard_map/while/body/eval_jaxpr/dot_general | solution.py:24
  75.0 3.2 %multiply_reduce_fusion.11 = f32[512]{0:T(512)S(1)} fusion(bf16[2048,512]{1,0:T(8,128)(2,1)} %get-tuple-element.733, f32[2048]{0:T(1024)S(1)} %mul.233, bf16[4,512,512]{2,1,0:T(8,128)(2,1)} %get-tuple-element.732, s32[]{:T(128)} %get-tuple-element.723), kind=kOutput, calls=%fused_computation.1.clone.1 | convolution fusion | flops 1077935616 | bytes 2632192 | tf_op jit(solution)/shard_map/while/body/eval_jaxpr/dot_general | solution.py:24
  78.5 3.2 %multiply_reduce_fusion.11 = f32[512]{0:T(512)S(1)} fusion(bf16[2048,512]{1,0:T(8,128)(2,1)} %get-tuple-element.733, f32[2048]{0:T(1024)S(1)} %mul.233, bf16[4,512,512]{2,1,0:T(8,128)(2,1)} %get-tuple-element.732, s32[]{:T(128)} %get-tuple-element.723), kind=kOutput, calls=%fused_computation.1.clone.1 | convolution fusion | flops 1077935616 | bytes 2632192 | tf_op jit(solution)/shard_map/while/body/eval_jaxpr/dot_general | solution.py:24
  81.9 3.2 %multiply_reduce_fusion.11 = f32[512]{0:T(512)S(1)} fusion(bf16[2048,512]{1,0:T(8,128)(2,1)} %get-tuple-element.733, f32[2048]{0:T(1024)S(1)} %mul.233, bf16[4,512,512]{2,1,0:T(8,128)(2,1)} %get-tuple-element.732, s32[]{:T(128)} %get-tuple-element.723), kind=kOutput, calls=%fused_computation.1.clone.1 | convolution fusion | flops 1077935616 | bytes 2632192 | tf_op jit(solution)/shard_map/while/body/eval_jaxpr/dot_general | solution.py:24
  85.2 33.0 %collective-permute-done = bf16[2048,512]{1,0:T(8,128)(2,1)} collective-permute-done((bf16[2048,512]{1,0:T(8,128)(2,1)}, bf16[2048,512]{1,0:T(8,128)(2,1)}, u32[]{:S(2)}, u32[]{:S(2)}) %collective-permute-start) | collective-permute-done | bytes 2097184 | tf_op jit(solution)/shard_map/ppermute | solution.py:14
  118.3 14.5 %while.59 = (s32[]{:T(128)}, f32[2048]{0:T(1024)S(1)}, f32[4,512]{1,0:T(4,128)S(1)}, bf16[4,512,512]{2,1,0:T(8,128)(2,1)}, bf16[2048,512]{1,0:T(8,128)(2,1)}, /*...) while((s32[]{:T(128)}, f32[2048]{0:T(1024)S(1)}, f32[4,512]{1,0:T(4,128)S(1)}, ...), condition=%wide.region_7.8_spmd.clone, body=%wide.region_4.7_spmd.clone.sunk | while | flops 1080034816 | bytes 2675311 | solution.py:34
  118.3 3.5 %multiply_reduce_fusion.12 = (f32[512]{0:T(512)S(1)}, f32[2048]{0:T(1024)S(1)}) fusion(f32[2048]{0:T(1024)S(1)} %get-tuple-element.761, f32[512]{0:T(512)S(1)} %bitcast.75, bf16[2048,512]{1,0:T(8,128)(2,1)} %get-tuple-element.759, bf16[4,512,512]{2,1,0:T(8,128)(2,1)} %get-tuple-element.758, s32[]{:T(128)} %get-tuple-element.746), kind=kOutput, calls=%fused_computation.7.clone.1 | convolution fusion | flops 1080030720 | bytes 2642432 | tf_op jit(solution)/shard_map/while/body/eval_jaxpr/dot_general | solution.py:24
  121.9 3.5 %multiply_reduce_fusion.12 = (f32[512]{0:T(512)S(1)}, f32[2048]{0:T(1024)S(1)}) fusion(f32[2048]{0:T(1024)S(1)} %get-tuple-element.761, f32[512]{0:T(512)S(1)} %bitcast.75, bf16[2048,512]{1,0:T(8,128)(2,1)} %get-tuple-element.759, bf16[4,512,512]{2,1,0:T(8,128)(2,1)} %get-tuple-element.758, s32[]{:T(128)} %get-tuple-element.746), kind=kOutput, calls=%fused_computation.7.clone.1 | convolution fusion | flops 1080030720 | bytes 2642432 | tf_op jit(solution)/shard_map/while/body/eval_jaxpr/dot_general | solution.py:24
  125.6 3.5 %multiply_reduce_fusion.12 = (f32[512]{0:T(512)S(1)}, f32[2048]{0:T(1024)S(1)}) fusion(f32[2048]{0:T(1024)S(1)} %get-tuple-element.761, f32[512]{0:T(512)S(1)} %bitcast.75, bf16[2048,512]{1,0:T(8,128)(2,1)} %get-tuple-element.759, bf16[4,512,512]{2,1,0:T(8,128)(2,1)} %get-tuple-element.758, s32[]{:T(128)} %get-tuple-element.746), kind=kOutput, calls=%fused_computation.7.clone.1 | convolution fusion | flops 1080030720 | bytes 2642432 | tf_op jit(solution)/shard_map/while/body/eval_jaxpr/dot_general | solution.py:24
  129.2 3.5 %multiply_reduce_fusion.12 = (f32[512]{0:T(512)S(1)}, f32[2048]{0:T(1024)S(1)}) fusion(f32[2048]{0:T(1024)S(1)} %get-tuple-element.761, f32[512]{0:T(512)S(1)} %bitcast.75, bf16[2048,512]{1,0:T(8,128)(2,1)} %get-tuple-element.759, bf16[4,512,512]{2,1,0:T(8,128)(2,1)} %get-tuple-element.758, s32[]{:T(128)} %get-tuple-element.746), kind=kOutput, calls=%fused_computation.7.clone.1 | convolution fusion | flops 1080030720 | bytes 2642432 | tf_op jit(solution)/shard_map/while/body/eval_jaxpr/dot_general | solution.py:24
  132.9 14.5 %while.60 = (s32[]{:T(128)}, f32[2048]{0:T(1024)S(1)}, f32[4,512]{1,0:T(4,128)S(1)}, bf16[4,512,512]{2,1,0:T(8,128)(2,1)}, bf16[2048,512]{1,0:T(8,128)(2,1)}, /*...) while((s32[]{:T(128)}, f32[2048]{0:T(1024)S(1)}, ...), condition=%wide.region_11.12_spmd.clone, body=%wide.region_8.11_spmd.clone.sunk | while | flops 1080034816 | bytes 2675311 | solution.py:34
  132.9 3.5 %multiply_reduce_fusion.13 = (f32[512]{0:T(512)S(1)}, f32[2048]{0:T(1024)S(1)}) fusion(f32[2048]{0:T(1024)S(1)} %get-tuple-element.713, f32[512]{0:T(512)S(1)} %bitcast.76, bf16[2048,512]{1,0:T(8,128)(2,1)} %get-tuple-element.711, bf16[4,512,512]{2,1,0:T(8,128)(2,1)} %get-tuple-element.710, s32[]{:T(128)} %get-tuple-element.698), kind=kOutput, calls=%fused_computation.16.clone.1 | convolution fusion | flops 1080030720 | bytes 2642432 | tf_op jit(solution)/shard_map/while/body/eval_jaxpr/dot_general | solution.py:24
  136.6 3.5 %multiply_reduce_fusion.13 = (f32[512]{0:T(512)S(1)}, f32[2048]{0:T(1024)S(1)}) fusion(f32[2048]{0:T(1024)S(1)} %get-tuple-element.713, f32[512]{0:T(512)S(1)} %bitcast.76, bf16[2048,512]{1,0:T(8,128)(2,1)} %get-tuple-element.711, bf16[4,512,512]{2,1,0:T(8,128)(2,1)} %get-tuple-element.710, s32[]{:T(128)} %get-tuple-element.698), kind=kOutput, calls=%fused_computation.16.clone.1 | convolution fusion | flops 1080030720 | bytes 2642432 | tf_op jit(solution)/shard_map/while/body/eval_jaxpr/dot_general | solution.py:24
  140.2 3.5 %multiply_reduce_fusion.13 = (f32[512]{0:T(512)S(1)}, f32[2048]{0:T(1024)S(1)}) fusion(f32[2048]{0:T(1024)S(1)} %get-tuple-element.713, f32[512]{0:T(512)S(1)} %bitcast.76, bf16[2048,512]{1,0:T(8,128)(2,1)} %get-tuple-element.711, bf16[4,512,512]{2,1,0:T(8,128)(2,1)} %get-tuple-element.710, s32[]{:T(128)} %get-tuple-element.698), kind=kOutput, calls=%fused_computation.16.clone.1 | convolution fusion | flops 1080030720 | bytes 2642432 | tf_op jit(solution)/shard_map/while/body/eval_jaxpr/dot_general | solution.py:24
  143.8 3.5 %multiply_reduce_fusion.13 = (f32[512]{0:T(512)S(1)}, f32[2048]{0:T(1024)S(1)}) fusion(f32[2048]{0:T(1024)S(1)} %get-tuple-element.713, f32[512]{0:T(512)S(1)} %bitcast.76, bf16[2048,512]{1,0:T(8,128)(2,1)} %get-tuple-element.711, bf16[4,512,512]{2,1,0:T(8,128)(2,1)} %get-tuple-element.710, s32[]{:T(128)} %get-tuple-element.698), kind=kOutput, calls=%fused_computation.16.clone.1 | convolution fusion | flops 1080030720 | bytes 2642432 | tf_op jit(solution)/shard_map/while/body/eval_jaxpr/dot_general | solution.py:24
  147.5 106.8 %collective-permute-done.6 = bf16[2048,512]{1,0:T(8,128)(2,1)S(1)} collective-permute-done((bf16[2048,512]{1,0:T(8,128)(2,1)}, bf16[2048,512]{1,0:T(8,128)(2,1)S(1)}, u32[]{:S(2)}, u32[]{:S(2)}) %collective-permute-start.6) | collective-permute-done | bytes 2097184 | tf_op jit(solution)/shard_map/ppermute | solution.py:14
  254.3 11.7 %while.61 = (s32[]{:T(128)}, f32[2048]{0:T(1024)S(1)}, f32[4,512]{1,0:T(4,128)S(1)}, bf16[4,512,512]{2,1,0:T(8,128)(2,1)}, bf16[2048,512]{1,0:T(8,128)(2,1)S(1)}...) while((s32[]{:T(128)}, f32[2048]{0:T(1024)S(1)}, ...), condition=%wide.region_15.16_spmd.clone, body=%wide.region_12.15_spmd.clone.sunk | while | flops 1080034816 | bytes 2675311 | solution.py:34
  254.3 2.8 %multiply_reduce_fusion.14 = (f32[512]{0:T(512)S(1)}, f32[2048]{0:T(1024)S(1)}) fusion(f32[2048]{0:T(1024)S(1)} %get-tuple-element.686, f32[512]{0:T(512)S(1)} %bitcast.77, bf16[2048,512]{1,0:T(8,128)(2,1)S(1)} %get-tuple-element.684, bf16[4,512,512]{2,1,0:T(8,128)(2,1)} %get-tuple-element.683, s32[]{:T(128)} %get-tuple-element.671), kind=kOutput, calls=%fused_computation.25.clone.1 | convolution fusion | flops 1080030720 | bytes 2642432 | tf_op jit(solution)/shard_map/while/body/eval_jaxpr/dot_general | solution.py:24
  257.2 2.8 %multiply_reduce_fusion.14 = (f32[512]{0:T(512)S(1)}, f32[2048]{0:T(1024)S(1)}) fusion(f32[2048]{0:T(1024)S(1)} %get-tuple-element.686, f32[512]{0:T(512)S(1)} %bitcast.77, bf16[2048,512]{1,0:T(8,128)(2,1)S(1)} %get-tuple-element.684, bf16[4,512,512]{2,1,0:T(8,128)(2,1)} %get-tuple-element.683, s32[]{:T(128)} %get-tuple-element.671), kind=kOutput, calls=%fused_computation.25.clone.1 | convolution fusion | flops 1080030720 | bytes 2642432 | tf_op jit(solution)/shard_map/while/body/eval_jaxpr/dot_general | solution.py:24
  260.2 2.8 %multiply_reduce_fusion.14 = (f32[512]{0:T(512)S(1)}, f32[2048]{0:T(1024)S(1)}) fusion(f32[2048]{0:T(1024)S(1)} %get-tuple-element.686, f32[512]{0:T(512)S(1)} %bitcast.77, bf16[2048,512]{1,0:T(8,128)(2,1)S(1)} %get-tuple-element.684, bf16[4,512,512]{2,1,0:T(8,128)(2,1)} %get-tuple-element.683, s32[]{:T(128)} %get-tuple-element.671), kind=kOutput, calls=%fused_computation.25.clone.1 | convolution fusion | flops 1080030720 | bytes 2642432 | tf_op jit(solution)/shard_map/while/body/eval_jaxpr/dot_general | solution.py:24
  263.1 2.8 %multiply_reduce_fusion.14 = (f32[512]{0:T(512)S(1)}, f32[2048]{0:T(1024)S(1)}) fusion(f32[2048]{0:T(1024)S(1)} %get-tuple-element.686, f32[512]{0:T(512)S(1)} %bitcast.77, bf16[2048,512]{1,0:T(8,128)(2,1)S(1)} %get-tuple-element.684, bf16[4,512,512]{2,1,0:T(8,128)(2,1)} %get-tuple-element.683, s32[]{:T(128)} %get-tuple-element.671), kind=kOutput, calls=%fused_computation.25.clone.1 | convolution fusion | flops 1080030720 | bytes 2642432 | tf_op jit(solution)/shard_map/while/body/eval_jaxpr/dot_general | solution.py:24
  266.2 3.3 %collective-permute-done.8 = f32[2048]{0:T(1024)S(1)} collective-permute-done((f32[2048]{0:T(1024)S(1)}, f32[2048]{0:T(1024)S(1)}, u32[]{:S(2)}, u32[]{:S(2)}) %collective-permute-start.8) | collective-permute-done | bytes 8224 | tf_op jit(solution)/shard_map/ppermute | solution.py:14
  (89 shorter events, 8.8 us)
Async XLA Ops:
  0.0 10.7 %copy-start = (bf16[2048,512]{1,0:T(8,128)(2,1)S(1)}, bf16[2048,512]{1,0:T(8,128)(2,1)}, u32[]{:S(2)}) copy-start(bf16[2048,512]{1,0:T(8,128)(2,1)} %param.10) | copy-start | bytes 6291460
  1.5 13.8 %all-to-all-start = ((s32[32,1,1]{2,1,0:T(1,128)}), s32[32,1,1]{2,1,0:T(1,128)S(1)}, u32[]{:S(2)}, u32[]{:S(2)}) async-start(s32[32,1,1]{2,1,0:T(1,128)} %copy.4), calls=%async_computation | async-start | bytes 32768 | tf_op jit(solution)/shard_map/all_to_all | solution.py:64
  15.3 53.7 %all-to-all-start.1 = ((bf16[32,64,512]{2,1,0:T(8,128)(2,1)}), bf16[32,64,512]{2,1,0:T(8,128)(2,1)}, u32[]{:S(2)}, u32[]{:S(2)}) async-start(bf16[32,64,512]{2,1,0:T(8,128)(2,1)} %bitcast.70), calls=%async_computation.1 | async-start | bytes 4194304 | tf_op jit(solution)/shard_map/all_to_all | solution.py:57
  20.0 37.9 %collective-permute-start.1 = (bf16[2048]{0:T(1024)(128)(2,1)S(1)}, bf16[2048]{0:T(1024)(128)(2,1)S(1)}, u32[]{:S(2)}, u32[]{:S(2)}) collective-permute-start(bf16[2048]{0:T(1024)(128)(2,1)S(1)} %convert_element_type.36), channel_id=1, source_target_pairs={{7,0},{0,1},{1,2},{2,3},{3,4},{4,5},{5,6},{6,7},{15,8},{8,9},{9,10... | collective-permute-start | bytes 12296 | tf_op jit(solution)/shard_map/ppermute | solution.py:14
  21.4 36.5 %collective-permute-start.4 = (bf16[2048]{0:T(1024)(128)(2,1)S(1)}, bf16[2048]{0:T(1024)(128)(2,1)S(1)}, u32[]{:S(2)}, u32[]{:S(2)}) collective-permute-start(bf16[2048]{0:T(1024)(128)(2,1)S(1)} %convert_element_type.36), channel_id=1, source_target_pairs={{6,0},{7,1},{0,2},{1,3},{2,4},{3,5},{4,6},{5,7},{14,8},{15,9},{8,1... | collective-permute-start | bytes 12296 | tf_op jit(solution)/shard_map/ppermute | solution.py:14
  22.7 45.9 %collective-permute-start.7 = (bf16[2048]{0:T(1024)(128)(2,1)S(1)}, bf16[2048]{0:T(1024)(128)(2,1)S(1)}, u32[]{:S(2)}, u32[]{:S(2)}) collective-permute-start(bf16[2048]{0:T(1024)(128)(2,1)S(1)} %convert_element_type.36), channel_id=1, source_target_pairs={{5,0},{6,1},{7,2},{0,3},{1,4},{2,5},{3,6},{4,7},{13,8},{14,9},{15,... | collective-permute-start | bytes 12296 | tf_op jit(solution)/shard_map/ppermute | solution.py:14
  69.0 49.3 %collective-permute-start = (bf16[2048,512]{1,0:T(8,128)(2,1)}, bf16[2048,512]{1,0:T(8,128)(2,1)}, u32[]{:S(2)}, u32[]{:S(2)}) collective-permute-start(bf16[2048,512]{1,0:T(8,128)(2,1)} %bitcast.3), channel_id=1, source_target_pairs={{7,0},{0,1},{1,2},{2,3},{3,4},{4,5},{5,6},{6,7},{15,8},{8,9},{9,10... | collective-permute-start | bytes 6291464 | tf_op jit(solution)/shard_map/ppermute | solution.py:14
  69.7 63.2 %collective-permute-start.3 = (bf16[2048,512]{1,0:T(8,128)(2,1)}, bf16[2048,512]{1,0:T(8,128)(2,1)}, u32[]{:S(2)}, u32[]{:S(2)}) collective-permute-start(bf16[2048,512]{1,0:T(8,128)(2,1)} %bitcast.3), channel_id=1, source_target_pairs={{6,0},{7,1},{0,2},{1,3},{2,4},{3,5},{4,6},{5,7},{14,8},{15,9},{8,1... | collective-permute-start | bytes 6291464 | tf_op jit(solution)/shard_map/ppermute | solution.py:14
  69.7 184.6 %collective-permute-start.6 = (bf16[2048,512]{1,0:T(8,128)(2,1)}, bf16[2048,512]{1,0:T(8,128)(2,1)S(1)}, u32[]{:S(2)}, u32[]{:S(2)}) collective-permute-start(bf16[2048,512]{1,0:T(8,128)(2,1)} %bitcast.3), channel_id=1, source_target_pairs={{5,0},{6,1},{7,2},{0,3},{1,4},{2,5},{3,6},{4,7},{13,8},{14,9},{15,... | collective-permute-start | bytes 6291464 | tf_op jit(solution)/shard_map/ppermute | solution.py:14
  132.8 133.3 %collective-permute-start.2 = (f32[2048]{0:T(1024)S(1)}, f32[2048]{0:T(1024)S(1)}, u32[]{:S(2)}, u32[]{:S(2)}) collective-permute-start(f32[2048]{0:T(1024)S(1)} %get-tuple-element.342), channel_id=1, source_target_pairs={{1,0},{2,1},{3,2},{4,3},{5,4},{6,5},{7,6},{0,7},{9,8},{10,9},{11,1... | collective-permute-start | bytes 24584 | tf_op jit(solution)/shard_map/ppermute | solution.py:14
  147.4 118.7 %collective-permute-start.5 = (f32[2048]{0:T(1024)S(1)}, f32[2048]{0:T(1024)S(1)}, u32[]{:S(2)}, u32[]{:S(2)}) collective-permute-start(f32[2048]{0:T(1024)S(1)} %get-tuple-element.344), channel_id=1, source_target_pairs={{2,0},{3,1},{4,2},{5,3},{6,4},{7,5},{0,6},{1,7},{10,8},{11,9},{12,... | collective-permute-start | bytes 24584 | tf_op jit(solution)/shard_map/ppermute | solution.py:14
  266.0 3.5 %collective-permute-start.8 = (f32[2048]{0:T(1024)S(1)}, f32[2048]{0:T(1024)S(1)}, u32[]{:S(2)}, u32[]{:S(2)}) collective-permute-start(f32[2048]{0:T(1024)S(1)} %get-tuple-element.346), channel_id=1, source_target_pairs={{3,0},{4,1},{5,2},{6,3},{7,4},{0,5},{1,6},{2,7},{11,8},{12,9},{13,... | collective-permute-start | bytes 24584 | tf_op jit(solution)/shard_map/ppermute | solution.py:14
where the time goes:
time: 273 us; the launch traced here: 270 us
  waiting for transfers between devices  190 us (70%)
  matrix products  52.6 us (19%)
  starting transfers between devices  18.3 us (7%)
  other arithmetic  5.65 us (2%)
  local copies, waits for them, and re-layouts  3.07 us (1%)
    ppermute x9, waiting for transfers between devices, shifted(): return lax.ppermute(block, axis, route)  187 us
    dot_general x16, matrix products, one_piece(): lax.dot_general(piece_block, right_rows, (((1,), (1,)), ((), ())), prefer...  52.6 us
    ppermute x9, starting transfers between devices, shifted(): return lax.ppermute(block, axis, route)  7.49 us
    all_to_all x1, starting transfers between devices, body(): lax.all_to_all(counts.reshape(nodes), ('gen', 'join'), split_axis=0, conc...  7.1 us
  transfers between devices with their start and end apart: 11, of which 7 were waited for; matrix products, arithmetic and copies ran while one was open for 22% of the time, Pallas kernels for 0%

commit v1 on v0

--- a/solution.py
+++ b/solution.py
@@ -3,9 +3,16 @@
 import jax
 import jax.numpy as jnp
 from jax import lax
+from jax.experimental import pallas as pl
+from jax.experimental.pallas import tpu as pltpu
 from jax.sharding import PartitionSpec as P
 
 ROUNDS = 3
+MESH = pl.DeviceIdType.MESH
+SCALE = 8.0 * math.log2(math.e)
+DEAD = -1e30
+LAYERS = 4
+OWN, YN, SIB, XN, XS = range(5)
 
 
 def shifted(block, axis, distance):
@@ -42,7 +49,7 @@
     return (row_sums.reshape(row_count), col_sums)
 
 
-def body(src_emb, counts):
+def ring_body(src_emb, counts):
     values = src_emb.astype(jnp.float32)
     width = values.shape[1]
     unit = (
@@ -77,7 +84,258 @@
     return live / (density + 1.0 - live)
 
 
+def layer_kernel(rows, width, src, flags, out, buf, snd, bias, acc, part, got, ws, wr,
+                 zsend, zrecv, lsend, lrecv, psem, wsend, wrecv):
+    gen, join = lax.axis_index("gen"), lax.axis_index("join")
+    x, k, z, y = gen // 2, gen % 2, join // 2, join % 2
+    zh, zl = z // 2, z % 2
+    layer = [z, 2 * zh + 1 - zl, 2 * (1 - zh) + zl, 3 - z]
+    nodes, joins = 32, 8
+    me = gen * joins + join
+    sibling = (2 * x + 1 - k, join)
+    x_near = (2 * (1 - x) + k, join)
+    y_near = (gen, 2 * z + 1 - y)
+    owners = 8
+    slots = rows // owners
+
+    barrier = pltpu.get_barrier_semaphore()
+
+    def greet(i, carry):
+        t = (me + i) % nodes
+        pl.semaphore_signal(barrier, inc=1, device_id=(t // joins, t % joins), device_id_type=MESH)
+        return carry
+
+    lax.fori_loop(1, nodes, greet, 0)
+
+    def normalize(d, into):
+        start = pl.multiple_of(layer[d] * rows, rows)
+        values = src[pl.ds(start, rows), :].astype(jnp.float32)
+        into[0:rows, :] = (
+            values
+            * lax.rsqrt(jnp.mean(values * values, axis=1, keepdims=True) + 1e-06)
+            / math.sqrt(width)
+        ).astype(jnp.bfloat16)
+        into[rows:rows + 16, :] = flags[layer[d]]
+
+    def z_copy(d):
+        return pltpu.make_async_remote_copy(
+            src_ref=snd.at[d - 1], dst_ref=buf.at[5 * d + OWN], send_sem=zsend.at[d - 1],
+            recv_sem=zrecv.at[d - 1], device_id=(gen, 2 * layer[d] + y), device_id_type=MESH,
+        )
+
+    def l_copy(d, kind):
+        source = XN if kind == XS else OWN
+        target = {SIB: sibling, XS: sibling, XN: x_near, YN: y_near}[kind]
+        return pltpu.make_async_remote_copy(
+            src_ref=buf.at[5 * d + source], dst_ref=buf.at[5 * d + kind],
+            send_sem=lsend.at[4 * d + kind - 1], recv_sem=lrecv.at[4 * d + kind - 1],
+            device_id=target, device_id_type=MESH,
+        )
+
+    def set_bias(d, kind):
+        slot = 4 * d + max(kind - 1, 0)
+        ones = jnp.full((16, 128), 1.0 / 16.0, jnp.bfloat16)
+        live = lax.dot_general(
+            buf[5 * d + kind, rows:rows + 16, :], ones, (((0,), (0,)), ((), ())),
+            preferred_element_type=jnp.float32,
+        )
+        bias[slot] = jnp.where(live > 0.5, -SCALE, DEAD)
+
+    piece = 128
+
+    def tile(row, row_slot, col, col_slot):
+        held = buf[row, 0:rows, :]
+        for b in range(rows // piece):
+            scores = lax.dot_general(
+                buf[col, b * piece:(b + 1) * piece, :], held, (((1,), (1,)), ((), ())),
+                preferred_element_type=jnp.float32,
+            )
+            shift = bias[col_slot, b * piece:(b + 1) * piece, :]
+            kernel = jnp.exp2(scores * SCALE + jnp.concatenate([shift] * (rows // 128), axis=1))
+            count = piece // slots
+            sums = jnp.sum(kernel.reshape(count, slots // 8, 8, rows), axis=1)
+            acc[row_slot, 8 * count * b:8 * count * (b + 1), :] += sums.reshape(8 * count, rows)
+
+    def over_rows(count, col, col_slot):
+        def step(i, carry):
+            tile(5 * (i // 2) + i % 2, i, col, col_slot)
+            return carry
+
+        lax.fori_loop(0, count, step, 0)
+
+    def over_cols(count, row, row_slot):
+        def step(i, carry):
+            c, kk = i // 4, i % 4
+            tile(row, row_slot, 5 * c + kk + (kk + 3) // 4, i)
+            return carry
+
+        lax.fori_loop(0, count, step, 0)
+
+    normalize(2, snd.at[1])
+    normalize(0, buf.at[OWN])
+    pl.semaphore_wait(barrier, nodes - 1)
+    z_copy(2).start()
+    l_copy(0, XN).start()
+    l_copy(0, YN).start()
+    l_copy(0, SIB).start()
+    normalize(1, snd.at[0])
+    z_copy(1).start()
+    normalize(3, snd.at[2])
+    z_copy(3).start()
+    acc[...] = jnp.zeros_like(acc)
+    part[...] = jnp.zeros_like(part)
+    ws[...] = jnp.zeros_like(ws)
+
+    def z_wait(d):
+        pltpu.make_async_remote_copy(
+            src_ref=snd.at[d - 1], dst_ref=buf.at[5 * d + OWN], send_sem=zsend.at[d - 1],
+            recv_sem=zrecv.at[d - 1], device_id=y_near, device_id_type=MESH,
+        ).wait_recv()
+
+    def phase(d, carry):
+        @pl.when(d > 0)
+        def _():
+            z_wait(d)
+            l_copy(d, XN).start()
+            l_copy(d, YN).start()
+            l_copy(d, SIB).start()
+
+        set_bias(d, OWN)
+        over_cols(4 * d, 5 * d + OWN, 2 * d)
+        over_rows(2 * d + 1, 5 * d + OWN, 4 * d)
+        l_copy(d, SIB).wait_recv()
+        set_bias(d, SIB)
+        over_rows(2 * d + 1, 5 * d + SIB, 4 * d + 1)
+        l_copy(d, XN).wait_recv()
+        l_copy(d, XS).start()
+        set_bias(d, XN)
+        over_rows(2 * d + 1, 5 * d + XN, 4 * d + 2)
+        l_copy(d, YN).wait_recv()
+        over_cols(4 * d + 3, 5 * d + YN, 2 * d + 1)
+        l_copy(d, XS).wait_recv()
+        set_bias(d, XS)
+        over_rows(2 * d + 2, 5 * d + XS, 4 * d + 3)
+        return carry
+
+    lax.fori_loop(0, LAYERS, phase, 0)
+
+    col_owner = lax.broadcasted_iota(jnp.int32, (8 * owners, rows), 0) // 8
+    row_owner = lax.broadcasted_iota(jnp.int32, (8 * owners, rows), 1) // slots
+    near = ((col_owner + 4) % owners != row_owner).astype(jnp.float32)
+
+    def total(i):
+        return jnp.sum(acc[i] * near, axis=0, keepdims=True)
+
+    for d in range(LAYERS):
+        part[d:d + 1, :] = total(2 * d + 1)
+    p_copy = pltpu.make_async_remote_copy(
+        src_ref=part, dst_ref=got, send_sem=psem.at[0], recv_sem=psem.at[1],
+        device_id=y_near, device_id_type=MESH,
+    )
+    p_copy.start()
+    mine = [total(2 * d) for d in range(LAYERS)]
+    p_copy.wait()
+    for d in range(LAYERS):
+        live = buf[5 * d + OWN, rows:rows + 16, :].astype(jnp.float32)[0:1, :]
+        weight = live / (mine[d] + got[d:d + 1, :] + 1.0 - live)
+        for j in range(owners):
+            ws[j, pl.ds(layer[d], 1), 0:slots] = weight[:, j * slots:(j + 1) * slots]
+
+    spot = 2 * gen + y
+
+    def w_copy(j):
+        return pltpu.make_async_remote_copy(
+            src_ref=ws.at[j], dst_ref=wr.at[spot], send_sem=wsend.at[j],
+            recv_sem=wrecv.at[spot], device_id=(z, j), device_id_type=MESH,
+        )
+
+    def w_got(i):
+        return pltpu.make_async_remote_copy(
+            src_ref=ws.at[0], dst_ref=wr.at[i], send_sem=wsend.at[0],
+            recv_sem=wrecv.at[i], device_id=y_near, device_id_type=MESH,
+        )
+
+    def send(j, carry):
+        @pl.when(z * joins + j != me)
+        def _():
+            w_copy(j).start()
+
+        @pl.when(z * joins + j == me)
+        def _():
+            wr[spot] = ws[j]
+
+        return carry
+
+    lax.fori_loop(0, owners, send, 0)
+
+    def receive(i, carry):
+        @pl.when((i // 2) * joins + 2 * gen + i % 2 != me)
+        def _():
+            w_got(i).wait_recv()
+
+        return carry
+
+    lax.fori_loop(0, owners, receive, 0)
+    out[...] = wr[...]
+
+    def sent(j, carry):
+        @pl.when(z * joins + j != me)
+        def _():
+            w_copy(j).wait_send()
+
+        return carry
+
+    lax.fori_loop(0, owners, sent, 0)
+    for d in range(1, LAYERS):
+        z_copy(d).wait_send()
+    for d in range(LAYERS):
+        for kind in (SIB, XN, YN, XS):
+            l_copy(d, kind).wait_send()
+
+
+def layer_body(src_emb, counts):
+    block, width = src_emb.shape
+    rows = block // LAYERS
+    owners = 8
+    slots = rows // owners
+    slot = lax.broadcasted_iota(jnp.int32, (LAYERS, 16, owners, slots), 3)
+    flags = (slot < counts.reshape(LAYERS, 1, owners, 1)).astype(jnp.bfloat16)
+    flags = flags.reshape(LAYERS, 16, rows)
+    vmem = pl.BlockSpec(memory_space=pltpu.VMEM)
+    weights = pl.pallas_call(
+        lambda *refs: layer_kernel(rows, width, *refs),
+        out_shape=jax.ShapeDtypeStruct((owners, 8, 128), jnp.float32),
+        in_specs=[vmem, vmem],
+        out_specs=vmem,
+        scratch_shapes=[
+            pltpu.VMEM((5 * LAYERS, rows + 16, width), jnp.bfloat16),
+            pltpu.VMEM((LAYERS - 1, rows + 16, width), jnp.bfloat16),
+            pltpu.VMEM((4 * LAYERS, rows, 128), jnp.float32),
+            pltpu.VMEM((2 * LAYERS, 8 * owners, rows), jnp.float32),
+            pltpu.VMEM((8, rows), jnp.float32),
+            pltpu.VMEM((8, rows), jnp.float32),
+            pltpu.VMEM((owners, 8, 128), jnp.float32),
+            pltpu.VMEM((owners, 8, 128), jnp.float32),
+            pltpu.SemaphoreType.DMA((LAYERS - 1,)),
+            pltpu.SemaphoreType.DMA((LAYERS - 1,)),
+            pltpu.SemaphoreType.DMA((4 * LAYERS,)),
+            pltpu.SemaphoreType.DMA((4 * LAYERS,)),
+            pltpu.SemaphoreType.DMA((2,)),
+            pltpu.SemaphoreType.DMA((owners,)),
+            pltpu.SemaphoreType.DMA((owners,)),
+        ],
+        compiler_params=pltpu.CompilerParams(
+            collective_id=0, has_side_effects=True, vmem_limit_bytes=56 * 2**20
+        ),
+        name="layer_kernel",
+    )(src_emb, flags)
+    weights = weights[:, :LAYERS, :slots].reshape(4, 2, LAYERS, slots)
+    return weights.transpose(0, 2, 1, 3).reshape(block)
+
+
 def solution(mesh):
     in_specs = (P(("gen", "join"), None), P(("gen", "join"), None))
     out_specs = P(("gen", "join"))
+    fits = mesh.shape["gen"] == 4 and mesh.shape["join"] == 8
+    body = layer_body if fits else ring_body
     return jax.shard_map(body, mesh=mesh, in_specs=in_specs, out_specs=out_specs, check_vma=False)

time: 273 us -> 152 us (0.56)
  waiting for transfers between devices: 190 us -> 0 us
  Pallas kernels: 0 us -> 147 us
  matrix products: 52.6 us -> 0 us
  starting transfers between devices: 18.3 us -> 0 us
  other arithmetic: 5.65 us -> 1.95 us
    ppermute x9 -> x0, waiting for transfers between devices: 187 us -> none  [shifted(): return lax.ppermute(block, axis, route)]
    pallas_call x0 -> x1, Pallas kernels: none -> 147 us  [layer_body(): pl.pallas_call(lambda *refs: layer_kernel(rows, width, *refs), out_shape=...]
    dot_general x16 -> x0, matrix products: 52.6 us -> none  [one_piece(): lax.dot_general(piece_block, right_rows, (((1,), (1,)), ((), ())), prefer...]
    all_to_all x2 -> x0, starting transfers between devices: 10.8 us -> none  [the longest x1 7.1 us: body(): lax.all_to_all(counts.reshape(nodes), ('gen', 'join'), split_axis=0, conc...]
    ppermute x9 -> x0, starting transfers between devices: 7.49 us -> none  [shifted(): return lax.ppermute(block, axis, route)]
    all_to_all x2 -> x0, waiting for transfers between devices: 3.19 us -> none  [the longest x1 2.76 us: body(): lax.all_to_all(counts.reshape(nodes), ('gen', 'join'), split_axis=0, conc...]
  transfers between devices with their start and end apart: 11 -> 0, of which waited for: 7 -> 0; matrix products, arithmetic and copies ran while one was open for 22% -> 0% of each run, Pallas kernels for 0% -> 0%
where the time goes in v1:
time: 152 us
  Pallas kernels  147 us (97%)
  local copies, waits for them, and re-layouts  2.28 us (1%)
  other arithmetic  1.95 us (1%)
    pallas_call x1, Pallas kernels, layer_body(): pl.pallas_call(lambda *refs: layer_kernel(rows, width, *refs), out_shape=...  147 us

profile of v1, /device:TPU:1, one launch (start us, length us, event | category | flops | bytes accessed | tf_op | source)
XLA Modules:
  0.0 151.6 jit_solution(14752322122386205971)
XLA Ops:
  0.0 0.5 broadcast.8
  0.5 1.3 reduce.3
  1.8 0.1 lt.15
  1.9 0.1 iota.12
  2.0 0.1 lt.16
  2.1 0.1 lt.17
  2.1 0.6 compare_convert_fusion.refs_1_
  2.8 147.4 %layer_kernel.1 = f32[8,8,128]{2,1,0:T(8,128)} custom-call(bf16[2048,512]{1,0:T(8,128)(2,1)} %refs_0_.1, bf16[4,16,512]{2,1,0:T(8,128)(2,1)} %compare_convert_fusion.refs_1_), custom_call_target="tpu_custom_call" | custom-call | tf_op jit(solution)/shard_map/layer_kernel/pallas_call | solution.py:305
  150.2 0.8 slice.3
  150.9 0.7 reshape.12
  (2 shorter events, 0.0 us)

commit v2 on v1

--- a/solution.py
+++ b/solution.py
@@ -84,7 +84,7 @@
     return live / (density + 1.0 - live)
 
 
-def layer_kernel(rows, width, src, flags, out, buf, snd, bias, acc, part, got, ws, wr,
+def layer_kernel(rows, width, src, flags, out, buf, snd, bias, mask, acc, cacc, ps, got, ws, wr,
                  zsend, zrecv, lsend, lrecv, psem, wsend, wrecv):
     gen, join = lax.axis_index("gen"), lax.axis_index("join")
     x, k, z, y = gen // 2, gen % 2, join // 2, join % 2
@@ -132,18 +132,28 @@
             device_id=target, device_id_type=MESH,
         )
 
+    lane_owner = lax.broadcasted_iota(jnp.int32, (owners, rows), 1) // slots
+    other_owner = (lax.broadcasted_iota(jnp.int32, (owners, rows), 0) + 4) % owners
+    near = (other_owner != lane_owner).astype(jnp.float32)
+
+    def at(kind):
+        return max(kind - 1, 0)
+
     def set_bias(d, kind):
-        slot = 4 * d + max(kind - 1, 0)
         ones = jnp.full((16, 128), 1.0 / 16.0, jnp.bfloat16)
         live = lax.dot_general(
             buf[5 * d + kind, rows:rows + 16, :], ones, (((0,), (0,)), ((), ())),
             preferred_element_type=jnp.float32,
         )
-        bias[slot] = jnp.where(live > 0.5, -SCALE, DEAD)
-
-    piece = 128
-
-    def tile(row, row_slot, col, col_slot):
+        bias[at(kind)] = jnp.where(live > 0.5, -SCALE, DEAD)
+
+    def set_mask(d, kind):
+        live = buf[5 * d + kind, rows:rows + 16, :].astype(jnp.float32)[0:owners, :]
+        mask[2 * d + kind] = live * near
+
+    piece = 256
+
+    def tile(row, slot, col, col_slot, both):
         held = buf[row, 0:rows, :]
         for b in range(rows // piece):
             scores = lax.dot_general(
@@ -153,23 +163,21 @@
             shift = bias[col_slot, b * piece:(b + 1) * piece, :]
             kernel = jnp.exp2(scores * SCALE + jnp.concatenate([shift] * (rows // 128), axis=1))
             count = piece // slots
-            sums = jnp.sum(kernel.reshape(count, slots // 8, 8, rows), axis=1)
-            acc[row_slot, 8 * count * b:8 * count * (b + 1), :] += sums.reshape(8 * count, rows)
-
-    def over_rows(count, col, col_slot):
+            kept = mask[slot, count * b:count * (b + 1), :]
+            kernel = (kernel.reshape(count, slots, rows) * kept[:, None, :]).reshape(piece, rows)
+            acc[slot] += jnp.sum(kernel.reshape(piece // 8, 8, rows), axis=0)
+            if both:
+                sums = kernel[:, 0:128]
+                for t in range(1, rows // 128):
+                    sums = sums + kernel[:, 128 * t:128 * (t + 1)]
+                cacc[col_slot, b * piece:(b + 1) * piece, :] += sums
+
+    def old_rows(d, kind):
         def step(i, carry):
-            tile(5 * (i // 2) + i % 2, i, col, col_slot)
+            tile(5 * (i // 2) + i % 2, i, 5 * d + kind, at(kind), True)
             return carry
 
-        lax.fori_loop(0, count, step, 0)
-
-    def over_cols(count, row, row_slot):
-        def step(i, carry):
-            c, kk = i // 4, i % 4
-            tile(row, row_slot, 5 * c + kk + (kk + 3) // 4, i)
-            return carry
-
-        lax.fori_loop(0, count, step, 0)
+        lax.fori_loop(0, 2 * d, step, 0)
 
     normalize(2, snd.at[1])
     normalize(0, buf.at[OWN])
@@ -183,7 +191,7 @@
     normalize(3, snd.at[2])
     z_copy(3).start()
     acc[...] = jnp.zeros_like(acc)
-    part[...] = jnp.zeros_like(part)
+    ps[...] = jnp.zeros_like(ps)
     ws[...] = jnp.zeros_like(ws)
 
     def z_wait(d):
@@ -193,51 +201,78 @@
         ).wait_recv()
 
     def phase(d, carry):
-        @pl.when(d > 0)
-        def _():
-            z_wait(d)
-            l_copy(d, XN).start()
-            l_copy(d, YN).start()
-            l_copy(d, SIB).start()
-
+        cacc[...] = jnp.zeros_like(cacc)
         set_bias(d, OWN)
-        over_cols(4 * d, 5 * d + OWN, 2 * d)
-        over_rows(2 * d + 1, 5 * d + OWN, 4 * d)
+        set_mask(d, OWN)
+        tile(5 * d + OWN, 2 * d, 5 * d + OWN, at(OWN), False)
+        old_rows(d, OWN)
         l_copy(d, SIB).wait_recv()
         set_bias(d, SIB)
-        over_rows(2 * d + 1, 5 * d + SIB, 4 * d + 1)
+        tile(5 * d + OWN, 2 * d, 5 * d + SIB, at(SIB), False)
+        old_rows(d, SIB)
         l_copy(d, XN).wait_recv()
         l_copy(d, XS).start()
+
+        @pl.when(d < LAYERS - 1)
+        def _():
+            z_wait(d + 1)
+            l_copy(d + 1, XN).start()
+            l_copy(d + 1, YN).start()
+            l_copy(d + 1, SIB).start()
+
         set_bias(d, XN)
-        over_rows(2 * d + 1, 5 * d + XN, 4 * d + 2)
+        tile(5 * d + OWN, 2 * d, 5 * d + XN, at(XN), False)
+        old_rows(d, XN)
         l_copy(d, YN).wait_recv()
-        over_cols(4 * d + 3, 5 * d + YN, 2 * d + 1)
+        set_mask(d, YN)
+
+        def new_row(kk, inner):
+            tile(5 * d + YN, 2 * d + 1, 5 * d + kk + (kk + 3) // 4, kk, False)
+            return inner
+
+        lax.fori_loop(0, 3, new_row, 0)
         l_copy(d, XS).wait_recv()
         set_bias(d, XS)
-        over_rows(2 * d + 2, 5 * d + XS, 4 * d + 3)
+        old_rows(d, XS)
+
+        def both_rows(kind, inner):
+            tile(5 * d + kind, 2 * d + kind, 5 * d + XS, at(XS), False)
+            return inner
+
+        lax.fori_loop(0, 2, both_rows, 0)
+        ones = jnp.ones((8, 128), jnp.float32)
+        for slot in range(4):
+            sums = lax.dot_general(
+                ones, cacc[slot], (((1,), (1,)), ((), ())),
+                preferred_element_type=jnp.float32, precision=lax.Precision.HIGHEST,
+            )
+            ps[slot, pl.ds(d, 1), :] = sums[0:1, :]
         return carry
 
     lax.fori_loop(0, LAYERS, phase, 0)
 
-    col_owner = lax.broadcasted_iota(jnp.int32, (8 * owners, rows), 0) // 8
-    row_owner = lax.broadcasted_iota(jnp.int32, (8 * owners, rows), 1) // slots
-    near = ((col_owner + 4) % owners != row_owner).astype(jnp.float32)
-
     def total(i):
-        return jnp.sum(acc[i] * near, axis=0, keepdims=True)
+        return jnp.sum(acc[i], axis=0, keepdims=True)
 
     for d in range(LAYERS):
-        part[d:d + 1, :] = total(2 * d + 1)
-    p_copy = pltpu.make_async_remote_copy(
-        src_ref=part, dst_ref=got, send_sem=psem.at[0], recv_sem=psem.at[1],
-        device_id=y_near, device_id_type=MESH,
-    )
-    p_copy.start()
+        ps[4, d:d + 1, :] = total(2 * d + 1)
+    x_sibling = (2 * (1 - x) + 1 - k, join)
+    p_copies = [
+        pltpu.make_async_remote_copy(
+            src_ref=ps.at[i], dst_ref=got.at[i - 1], send_sem=psem.at[i - 1],
+            recv_sem=psem.at[3 + i], device_id=target, device_id_type=MESH,
+        )
+        for i, target in ((1, sibling), (2, x_near), (3, x_sibling), (4, y_near))
+    ]
+    for copy in p_copies:
+        copy.start()
     mine = [total(2 * d) for d in range(LAYERS)]
-    p_copy.wait()
+    for copy in p_copies:
+        copy.wait()
+    sums = ps[0] + got[0] + got[1] + got[2] + got[3]
     for d in range(LAYERS):
         live = buf[5 * d + OWN, rows:rows + 16, :].astype(jnp.float32)[0:1, :]
-        weight = live / (mine[d] + got[d:d + 1, :] + 1.0 - live)
+        weight = live / (mine[d] + sums[d:d + 1, :] + 1.0 - live)
         for j in range(owners):
             ws[j, pl.ds(layer[d], 1), 0:slots] = weight[:, j * slots:(j + 1) * slots]
 
@@ -310,17 +345,19 @@
         scratch_shapes=[
             pltpu.VMEM((5 * LAYERS, rows + 16, width), jnp.bfloat16),
             pltpu.VMEM((LAYERS - 1, rows + 16, width), jnp.bfloat16),
-            pltpu.VMEM((4 * LAYERS, rows, 128), jnp.float32),
-            pltpu.VMEM((2 * LAYERS, 8 * owners, rows), jnp.float32),
-            pltpu.VMEM((8, rows), jnp.float32),
-            pltpu.VMEM((8, rows), jnp.float32),
+            pltpu.VMEM((4, rows, 128), jnp.float32),
+            pltpu.VMEM((2 * LAYERS, owners, rows), jnp.float32),
+            pltpu.VMEM((2 * LAYERS, 8, rows), jnp.float32),
+            pltpu.VMEM((4, rows, 128), jnp.float32),
+            pltpu.VMEM((5, 8, rows), jnp.float32),
+            pltpu.VMEM((4, 8, rows), jnp.float32),
             pltpu.VMEM((owners, 8, 128), jnp.float32),
             pltpu.VMEM((owners, 8, 128), jnp.float32),
             pltpu.SemaphoreType.DMA((LAYERS - 1,)),
             pltpu.SemaphoreType.DMA((LAYERS - 1,)),
             pltpu.SemaphoreType.DMA((4 * LAYERS,)),
             pltpu.SemaphoreType.DMA((4 * LAYERS,)),
-            pltpu.SemaphoreType.DMA((2,)),
+            pltpu.SemaphoreType.DMA((8,)),
             pltpu.SemaphoreType.DMA((owners,)),
             pltpu.SemaphoreType.DMA((owners,)),
         ],

time: 152 us -> 96.8 us (0.64)
  Pallas kernels: 147 us -> 92.4 us
    pallas_call x1, Pallas kernels: 147 us -> 92.4 us  [layer_body(): pl.pallas_call(lambda *refs: layer_kernel(rows, width, *refs), out_shape=...]
where the time goes in v2:
time: 96.8 us; the launch traced here: 96.6 us
  Pallas kernels  92.4 us (95%)
  local copies, waits for them, and re-layouts  2.28 us (2%)
  other arithmetic  1.95 us (2%)
    pallas_call x1, Pallas kernels, layer_body(): pl.pallas_call(lambda *refs: layer_kernel(rows, width, *refs), out_shape=...  92.4 us

profile of v2, /device:TPU:1, one launch (start us, length us, event | category | flops | bytes accessed | tf_op | source)
XLA Modules:
  0.0 96.6 jit_solution(6497591873607478562)
XLA Ops:
  0.0 0.5 broadcast.8
  0.5 1.3 %reduce.3 = s32[32]{0:T(128)S(1)} reduce(s32[1,32]{1,0:T(1,128)} %param.3, s32[]{:T(128)} %broadcast.8), dimensions={0}, to_apply=%param.3.reduce_sub_computation.3 | reduce | bytes 260 | tf_op args[1]
  1.8 0.1 lt.15
  1.9 0.1 iota.12
  2.0 0.1 lt.16
  2.1 0.1 lt.17
  2.1 0.6 compare_convert_fusion.refs_1_
  2.8 92.4 %layer_kernel.1 = f32[8,8,128]{2,1,0:T(8,128)} custom-call(bf16[2048,512]{1,0:T(8,128)(2,1)} %refs_0_.1, bf16[4,16,512]{2,1,0:T(8,128)(2,1)} %compare_convert_fusion.refs_1_), custom_call_target="tpu_custom_call" | custom-call | tf_op jit(solution)/shard_map/layer_kernel/pallas_call | solution.py:340
  95.1 0.8 slice.3
  95.9 0.7 reshape.12
  (2 shorter events, 0.0 us)

commit v3 on v2

--- a/solution.py
+++ b/solution.py
@@ -117,20 +117,36 @@
         ).astype(jnp.bfloat16)
         into[rows:rows + 16, :] = flags[layer[d]]
 
-    def z_copy(d):
+    halves = (pl.ds(0, rows // 2), pl.ds(rows // 2, rows // 2 + 16))
+
+    def z_copy(d, h):
         return pltpu.make_async_remote_copy(
-            src_ref=snd.at[d - 1], dst_ref=buf.at[5 * d + OWN], send_sem=zsend.at[d - 1],
-            recv_sem=zrecv.at[d - 1], device_id=(gen, 2 * layer[d] + y), device_id_type=MESH,
-        )
-
-    def l_copy(d, kind):
+            src_ref=snd.at[d - 1, halves[h]], dst_ref=buf.at[5 * d + OWN, halves[h]],
+            send_sem=zsend.at[2 * d - 2 + h], recv_sem=zrecv.at[2 * d - 2 + h],
+            device_id=(gen, 2 * layer[d] + y), device_id_type=MESH,
+        )
+
+    def l_copy(d, kind, h):
         source = XN if kind == XS else OWN
         target = {SIB: sibling, XS: sibling, XN: x_near, YN: y_near}[kind]
+        sem = 2 * (4 * d + kind - 1) + h
         return pltpu.make_async_remote_copy(
-            src_ref=buf.at[5 * d + source], dst_ref=buf.at[5 * d + kind],
-            send_sem=lsend.at[4 * d + kind - 1], recv_sem=lrecv.at[4 * d + kind - 1],
+            src_ref=buf.at[5 * d + source, halves[h]], dst_ref=buf.at[5 * d + kind, halves[h]],
+            send_sem=lsend.at[sem], recv_sem=lrecv.at[sem],
             device_id=target, device_id_type=MESH,
         )
+
+    def z_start(d):
+        for h in range(2):
+            z_copy(d, h).start()
+
+    def l_start(d, h):
+        for kind in (XN, YN, SIB):
+            l_copy(d, kind, h).start()
+
+    def l_wait(d, kind):
+        for h in range(2):
+            l_copy(d, kind, h).wait_recv()
 
     lane_owner = lax.broadcasted_iota(jnp.int32, (owners, rows), 1) // slots
     other_owner = (lax.broadcasted_iota(jnp.int32, (owners, rows), 0) + 4) % owners
@@ -174,30 +190,31 @@
 
     def old_rows(d, kind):
         def step(i, carry):
-            tile(5 * (i // 2) + i % 2, i, 5 * d + kind, at(kind), True)
+            for own_or_yn in range(2):
+                tile(5 * i + own_or_yn, 2 * i + own_or_yn, 5 * d + kind, at(kind), True)
             return carry
 
-        lax.fori_loop(0, 2 * d, step, 0)
+        lax.fori_loop(0, d, step, 0)
 
     normalize(2, snd.at[1])
     normalize(0, buf.at[OWN])
     pl.semaphore_wait(barrier, nodes - 1)
-    z_copy(2).start()
-    l_copy(0, XN).start()
-    l_copy(0, YN).start()
-    l_copy(0, SIB).start()
+    z_start(2)
+    l_start(0, 0)
+    l_start(0, 1)
     normalize(1, snd.at[0])
-    z_copy(1).start()
+    z_start(1)
     normalize(3, snd.at[2])
-    z_copy(3).start()
+    z_start(3)
     acc[...] = jnp.zeros_like(acc)
     ps[...] = jnp.zeros_like(ps)
     ws[...] = jnp.zeros_like(ws)
 
-    def z_wait(d):
+    def z_wait(d, h):
         pltpu.make_async_remote_copy(
-            src_ref=snd.at[d - 1], dst_ref=buf.at[5 * d + OWN], send_sem=zsend.at[d - 1],
-            recv_sem=zrecv.at[d - 1], device_id=y_near, device_id_type=MESH,
+            src_ref=snd.at[d - 1, halves[h]], dst_ref=buf.at[5 * d + OWN, halves[h]],
+            send_sem=zsend.at[2 * d - 2 + h], recv_sem=zrecv.at[2 * d - 2 + h],
+            device_id=y_near, device_id_type=MESH,
         ).wait_recv()
 
     def phase(d, carry):
@@ -206,24 +223,24 @@
         set_mask(d, OWN)
         tile(5 * d + OWN, 2 * d, 5 * d + OWN, at(OWN), False)
         old_rows(d, OWN)
-        l_copy(d, SIB).wait_recv()
+        l_wait(d, SIB)
         set_bias(d, SIB)
         tile(5 * d + OWN, 2 * d, 5 * d + SIB, at(SIB), False)
         old_rows(d, SIB)
-        l_copy(d, XN).wait_recv()
-        l_copy(d, XS).start()
-
-        @pl.when(d < LAYERS - 1)
-        def _():
-            z_wait(d + 1)
-            l_copy(d + 1, XN).start()
-            l_copy(d + 1, YN).start()
-            l_copy(d + 1, SIB).start()
+        for h in range(2):
+            l_copy(d, XN, h).wait_recv()
+            l_copy(d, XS, h).start()
+
+        @pl.when(d < LAYERS - 2)
+        def _():
+            for h in range(2):
+                z_wait(d + 1, h)
+                l_start(d + 1, h)
 
         set_bias(d, XN)
         tile(5 * d + OWN, 2 * d, 5 * d + XN, at(XN), False)
         old_rows(d, XN)
-        l_copy(d, YN).wait_recv()
+        l_wait(d, YN)
         set_mask(d, YN)
 
         def new_row(kk, inner):
@@ -231,15 +248,19 @@
             return inner
 
         lax.fori_loop(0, 3, new_row, 0)
-        l_copy(d, XS).wait_recv()
+        @pl.when(d == LAYERS - 2)
+        def _():
+            for h in range(2):
+                z_wait(d + 1, h)
+                l_start(d + 1, h)
+
+        l_wait(d, XS)
         set_bias(d, XS)
         old_rows(d, XS)
 
-        def both_rows(kind, inner):
+        for kind in (OWN, YN):
             tile(5 * d + kind, 2 * d + kind, 5 * d + XS, at(XS), False)
-            return inner
-
-        lax.fori_loop(0, 2, both_rows, 0)
+
         ones = jnp.ones((8, 128), jnp.float32)
         for slot in range(4):
             sums = lax.dot_general(
@@ -322,10 +343,12 @@
 
     lax.fori_loop(0, owners, sent, 0)
     for d in range(1, LAYERS):
-        z_copy(d).wait_send()
+        for h in range(2):
+            z_copy(d, h).wait_send()
     for d in range(LAYERS):
         for kind in (SIB, XN, YN, XS):
-            l_copy(d, kind).wait_send()
+            for h in range(2):
+                l_copy(d, kind, h).wait_send()
 
 
 def layer_body(src_emb, counts):
@@ -353,10 +376,10 @@
             pltpu.VMEM((4, 8, rows), jnp.float32),
             pltpu.VMEM((owners, 8, 128), jnp.float32),
             pltpu.VMEM((owners, 8, 128), jnp.float32),
-            pltpu.SemaphoreType.DMA((LAYERS - 1,)),
-            pltpu.SemaphoreType.DMA((LAYERS - 1,)),
-            pltpu.SemaphoreType.DMA((4 * LAYERS,)),
-            pltpu.SemaphoreType.DMA((4 * LAYERS,)),
+            pltpu.SemaphoreType.DMA((2 * LAYERS - 2,)),
+            pltpu.SemaphoreType.DMA((2 * LAYERS - 2,)),
+            pltpu.SemaphoreType.DMA((8 * LAYERS,)),
+            pltpu.SemaphoreType.DMA((8 * LAYERS,)),
             pltpu.SemaphoreType.DMA((8,)),
             pltpu.SemaphoreType.DMA((owners,)),
             pltpu.SemaphoreType.DMA((owners,)),

time: 96.8 us -> 89 us (0.919)
  Pallas kernels: 92.4 us -> 84.5 us
    pallas_call x1, Pallas kernels: 92.4 us -> 84.5 us  [layer_body(): pl.pallas_call(lambda *refs: layer_kernel(rows, width, *refs), out_shape=...]
where the time goes in v3:
time: 89 us; the launch traced here: 88.8 us
  Pallas kernels  84.5 us (95%)
  local copies, waits for them, and re-layouts  2.28 us (3%)
  other arithmetic  1.95 us (2%)
    pallas_call x1, Pallas kernels, layer_body(): pl.pallas_call(lambda *refs: layer_kernel(rows, width, *refs), out_shape=...  84.5 us

profile of v3, /device:TPU:1, one launch (start us, length us, event | category | flops | bytes accessed | tf_op | source)
XLA Modules:
  0.0 88.8 jit_solution(9757557372708871185)
XLA Ops:
  0.0 0.5 broadcast.8
  0.5 1.3 %reduce.3 = s32[32]{0:T(128)S(1)} reduce(s32[1,32]{1,0:T(1,128)} %param.3, s32[]{:T(128)} %broadcast.8), dimensions={0}, to_apply=%param.3.reduce_sub_computation.3 | reduce | bytes 260 | tf_op args[1]
  1.8 0.1 lt.15
  1.9 0.1 iota.12
  2.0 0.1 lt.16
  2.1 0.1 lt.17
  2.1 0.6 compare_convert_fusion.refs_1_
  2.8 84.5 %layer_kernel.1 = f32[8,8,128]{2,1,0:T(8,128)} custom-call(bf16[2048,512]{1,0:T(8,128)(2,1)} %refs_0_.1, bf16[4,16,512]{2,1,0:T(8,128)(2,1)} %compare_convert_fusion.refs_1_), custom_call_target="tpu_custom_call" | custom-call | tf_op jit(solution)/shard_map/layer_kernel/pallas_call | solution.py:363
  87.3 0.8 slice.3
  88.1 0.7 reshape.12
  (2 shorter events, 0.0 us)
